TPU v7x, 256 devices: a whole 4x4x8 slice. The times are simulated.
256 devices in a mesh: section: 8 (over y, core), ctx: 32 (over z, x).
Axes of the slice: x: 4, y: 4, z: 8, core: 2. Of those that a mesh axis runs over, the one named last changes fastest.
Arguments:
- section_input: bfloat16 [2, 4096, 2048], P(None, 'ctx'), may hold values from -6 to 6
- cotangent: bfloat16 [2, 4096, 2048], P(None, 'ctx'), may hold values from -6 to 6
- w_query: bfloat16 [8, 2048, 1024], P('section', 'ctx'), may hold values from -0.125 to 0.125
- w_key: bfloat16 [8, 2048, 1024], P('section', 'ctx'), may hold values from -0.125 to 0.125
- w_value: bfloat16 [8, 2048, 1024], P('section', 'ctx'), may hold values from -0.125 to 0.125
- w_out: bfloat16 [8, 1024, 2048], P('section', 'ctx'), may hold values from -0.1875 to 0.1875
- block_mask: int32 [2, 128, 2], P(None, 'ctx'), may hold values 0 or 1
Outputs:
- section_output: bfloat16 [8, 2, 4096, 2048], P('section', None, 'ctx')
- input_grad: bfloat16 [8, 2, 4096, 2048], P('section', None, 'ctx')
Inputs may be any that keep to these rules, and one draw needn't show every extreme that they name: A block always attends to itself; column 0 and 1 of block_mask choose its two neighbour blocks.
All inputs are finite; a program needn't handle non-finite values.
Results may differ from a plain program's by a relative error of at most 0.03.
Values may be sent and summed in bfloat16 or wider, within the bound.
No kernel may reach another device: no remote copies, remote signals or barrier semaphores. Data moves between devices by JAX's collectives and lax.ppermute only.
A program may use at most 128 MiB of HBM per device.

v0:
```python
import jax
import jax.numpy as jnp
from jax import lax
from jax.sharding import PartitionSpec as P

D = 2048
HEADS = 8
HDIM = 128
BLOCKS_DEV = 4
BLK = 32


def padded(block, sides, width):
    for axis, dim in sides:
        count = lax.axis_size(axis)
        forward = [(i, i + 1) for i in range(count - 1)]
        backward = [(target, source) for source, target in forward]
        low = lax.ppermute(
            lax.slice_in_dim(block, block.shape[dim] - width, None, axis=dim), axis, forward
        )
        high = lax.ppermute(lax.slice_in_dim(block, 0, width, axis=dim), axis, backward)
        block = jnp.concatenate([low, block, high], axis=dim)
    return block


def shifted(block, axis, distance):
    devices = range(lax.axis_size(axis))
    route = [(i - distance, i) for i in devices if i - distance in devices]
    return lax.ppermute(block, axis, route)


def rms_scale(values):
    return values * lax.rsqrt(jnp.mean(values * values, axis=-1, keepdims=True) + 1e-06)


def allowed_keys(mask_rows, block_ids, block_count):
    mask_float = mask_rows.astype(jnp.float32)
    left = mask_float[:, 0] * (block_ids > 0).astype(jnp.float32)
    right = mask_float[:, 1] * (block_ids < block_count - 1).astype(jnp.float32)
    return jnp.stack([left, jnp.ones_like(left), right], axis=1)


def project(layer_in, w_query, w_key, w_value):
    length = layer_in.shape[0]
    normed = rms_scale(layer_in.astype(jnp.float32)).astype(jnp.bfloat16)

    def head_normed(weight):
        out = jnp.dot(normed, weight, preferred_element_type=jnp.float32)
        out = rms_scale(out.reshape(length, HEADS, HDIM))
        return out.reshape(length, HEADS * HDIM).astype(jnp.bfloat16)

    query = head_normed(w_query)
    key = head_normed(w_key)
    value = jnp.dot(normed, w_value, preferred_element_type=jnp.float32).astype(jnp.bfloat16)
    return (query, key, value)


def attend(query, keys_ext, values_ext, allow, layer_in, w_out):
    length = query.shape[0]
    nblock = length // BLK
    queries = query.reshape(nblock, BLK, HEADS, HDIM)

    def windows(extended):
        grid = extended.reshape(nblock + 2, BLK, HEADS, HDIM)
        return jnp.concatenate([grid[:-2], grid[1:-1], grid[2:]], axis=1)

    keys = windows(keys_ext)
    values = windows(values_ext)
    scores = jnp.einsum(
        "bqhd,bkhd->bhqk", queries, keys, preferred_element_type=jnp.float32
    ) * HDIM ** (-0.5)
    weight = jnp.repeat(allow, BLK, axis=1)[:, None, None, :]
    probs = jnp.exp(scores) * weight
    total = jnp.sum(probs, axis=-1)
    attended = jnp.einsum(
        "bhqk,bkhd->bqhd", probs.astype(jnp.bfloat16), values, preferred_element_type=jnp.float32
    )
    attended = attended / jnp.transpose(total, (0, 2, 1))[..., None]
    attended = attended.reshape(length, HEADS * HDIM).astype(jnp.bfloat16)
    update = jnp.dot(attended, w_out, preferred_element_type=jnp.float32)
    return (layer_in.astype(jnp.float32) + update).astype(jnp.bfloat16)


def put_slot(buffer, value, slot, active):
    return jnp.where(active, lax.dynamic_update_index_in_dim(buffer, value, slot, 0), buffer)


def take_slot(buffer, slot):
    return lax.dynamic_index_in_dim(buffer, slot, 0, keepdims=False)


def per_device(section_input, cotangent, w_query, w_key, w_value, w_out, block_mask):
    n_section = lax.axis_size("section")
    n_ctx = lax.axis_size("ctx")
    section = lax.axis_index("section")
    place = lax.axis_index("ctx")
    micro = section_input.shape[0]
    length = section_input.shape[1]
    width = HEADS * HDIM
    full_query, full_key, full_value, full_out = (
        lax.all_gather(w_query[0], "ctx", axis=0, tiled=True),
        lax.all_gather(w_key[0], "ctx", axis=0, tiled=True),
        lax.all_gather(w_value[0], "ctx", axis=0, tiled=True),
        lax.all_gather(w_out[0], "ctx", axis=0, tiled=True),
    )
    block_ids = place * BLOCKS_DEV + jnp.arange(BLOCKS_DEV)
    allows = jax.vmap(lambda rows_mask: allowed_keys(rows_mask, block_ids, BLOCKS_DEV * n_ctx))(
        block_mask
    )
    zero_rows = jnp.zeros((length, D), jnp.bfloat16)
    zero_heads = jnp.zeros((length, width), jnp.bfloat16)
    zero_wide = jnp.zeros((length + 2 * BLK, width), jnp.bfloat16)
    steps_total = n_section + micro - 1

    def run_project(values):
        return project(values, full_query, full_key, full_value)

    def skip_project(values):
        return (zero_heads, zero_heads, zero_heads)

    def run_attend(query, extended, layer_in, allow):
        return attend(query, extended[0], extended[1], allow, layer_in, full_out)

    def skip_attend(query, extended, layer_in, allow):
        return zero_rows

    kv_store = jnp.zeros((micro, 2, length, width), jnp.bfloat16)
    inputs = jnp.zeros((micro, length, D), jnp.bfloat16)
    outputs = jnp.zeros((micro, length, D), jnp.bfloat16)
    queries = jnp.zeros((micro, length, width), jnp.bfloat16)

    def forward_step(step, carry):
        incoming, inputs, outputs, queries, kv_store = carry
        micro_id = step - section
        active = (micro_id >= 0) & (micro_id < micro)
        slot = jnp.clip(micro_id, 0, micro - 1)
        layer_in = jnp.where(section == 0, take_slot(section_input, slot), incoming)
        query, key, value = lax.cond(active, run_project, skip_project, layer_in)
        local_kv = jnp.stack([key, value])
        extended = padded(local_kv, (("ctx", 1),), BLK)
        allow = take_slot(allows, slot)
        result = lax.cond(active, run_attend, skip_attend, query, extended, layer_in, allow)
        inputs = put_slot(inputs, layer_in, slot, active)
        outputs = put_slot(outputs, result, slot, active)
        queries = put_slot(queries, query, slot, active)
        kv_store = put_slot(kv_store, local_kv, slot, active)
        incoming = shifted(result, "section", 1)
        return (incoming, inputs, outputs, queries, kv_store)

    carry = (zero_rows, inputs, outputs, queries, kv_store)
    _, inputs, outputs, queries, kv_store = lax.fori_loop(0, steps_total, forward_step, carry)

    def pull_attend(query, extended, layer_in, allow, grad_in):

        def local_attend(query_in, keys_in, values_in, rows_in):
            return attend(query_in, keys_in, values_in, allow, rows_in, full_out)

        _, pull = jax.vjp(local_attend, query, extended[0], extended[1], layer_in)
        return pull(grad_in)

    def skip_pull(query, extended, layer_in, allow, grad_in):
        return (zero_heads, zero_wide, zero_wide, zero_rows)

    def pull_project(layer_in, d_query, own):
        _, pull = jax.vjp(run_project, layer_in)
        return pull((d_query, own[0], own[1]))[0]

    def skip_pull_project(layer_in, d_query, own):
        return zero_rows

    grads = jnp.zeros((micro, length, D), jnp.bfloat16)

    def backward_step(step, carry):
        incoming, grads = carry
        micro_id = step - (n_section - 1 - section)
        active = (micro_id >= 0) & (micro_id < micro)
        slot = jnp.clip(micro_id, 0, micro - 1)
        grad_in = jnp.where(section == n_section - 1, take_slot(cotangent, slot), incoming)
        layer_in = take_slot(inputs, slot)
        query = take_slot(queries, slot)
        extended = padded(take_slot(kv_store, slot), (("ctx", 1),), BLK)
        allow = take_slot(allows, slot)
        d_query, d_keys, d_values, d_direct = lax.cond(
            active, pull_attend, skip_pull, query, extended, layer_in, allow, grad_in
        )
        d_wide = jnp.stack([d_keys, d_values])
        rims = jnp.concatenate([d_wide[:, :BLK], d_wide[:, -BLK:]], axis=1)
        returned = padded(rims, (("ctx", 1),), BLK)
        own = d_wide[:, BLK:-BLK]
        own = own.at[:, :BLK].add(returned[:, :BLK])
        own = own.at[:, -BLK:].add(returned[:, -BLK:])
        d_projected = lax.cond(active, pull_project, skip_pull_project, layer_in, d_query, own)
        d_input = d_direct + d_projected
        grads = put_slot(grads, d_input, slot, active)
        incoming = shifted(d_input, "section", -1)
        return (incoming, grads)

    _, grads = lax.fori_loop(0, steps_total, backward_step, (zero_rows, grads))
    return (outputs[None], grads[None])


def solution(mesh):
    return jax.shard_map(
        per_device,
        mesh=mesh,
        in_specs=(
            P(None, "ctx", None),
            P(None, "ctx", None),
            P("section", "ctx", None),
            P("section", "ctx", None),
            P("section", "ctx", None),
            P("section", "ctx", None),
            P(None, "ctx", None),
        ),
        out_specs=(P("section", None, "ctx", None), P("section", None, "ctx", None)),
        check_vma=False,
    )
```

profile of v0, /device:TPU:103, one launch (start us, length us, event | category | flops | bytes accessed | tf_op | source)
XLA Modules:
  0.0 1315.3 jit_solution(2852460559565105699)
XLA Ops:
  11.0 78.0 %all-gather.9.cloned.1.call-done = bf16[1,2048,1024]{2,1,0:T(8,128)(2,1)} async-done(((bf16[1,64,1024]{2,1,0:T(8,128)(2,1)}), bf16[1,2048,1024]{2,1,0:T(8,128)(2,1)}) %all-gather.9.cloned.1.call-update) | async-done | bytes 4194320 | tf_op jit(solution)/shard_map/all_gather | solution.py:101
  88.9 81.8 %all-gather.11.cloned.1.call-done = bf16[1,2048,1024]{2,1,0:T(8,128)(2,1)} async-done(((bf16[1,64,1024]{2,1,0:T(8,128)(2,1)}), bf16[1,2048,1024]{2,1,0:T(8,128)(2,1)}) %all-gather.11.cloned.1.call-update) | async-done | bytes 4194320 | tf_op jit(solution)/shard_map/all_gather | solution.py:102
  170.7 81.8 %all-gather.13.cloned.1.call-done = bf16[1,2048,1024]{2,1,0:T(8,128)(2,1)} async-done(((bf16[1,64,1024]{2,1,0:T(8,128)(2,1)}), bf16[1,2048,1024]{2,1,0:T(8,128)(2,1)}) %all-gather.13.cloned.1.call-update) | async-done | bytes 4194320 | tf_op jit(solution)/shard_map/all_gather | solution.py:103
  252.5 81.6 %all-gather.15.cloned.1.call-done = bf16[1,1024,2048]{2,1,0:T(8,128)(2,1)} async-done(((bf16[1,32,2048]{2,1,0:T(8,128)(2,1)}), bf16[1,1024,2048]{2,1,0:T(8,128)(2,1)}) %all-gather.15.cloned.1.call-update) | async-done | bytes 4194320 | tf_op jit(solution)/shard_map/all_gather | solution.py:104
  337.4 301.7 %while.41 = (s32[]{:T(128)}, bf16[128,2048]{1,0:T(8,128)(2,1)S(1)}, bf16[2,128,2048]{2,1,0:T(8,128)(2,1)S(1)}, bf16[2,128,2048]{2,1,0:T(8,128)(2,1)}, bf16[2,128...) while((s32[]{:T(128)}, bf16[128,2048]{1,0:T(8,128)(2,1)S(1)}, ...), condition=%wide.region_9.10_spmd, body=%wide.region_0.9_spmd.sunk | while | flops 2211841024 | bytes 75189416 | solution.py:151
  362.1 12.5 collective-permute-done.2
  376.0 10.8 conditional.8
  414.6 10.8 conditional.8
  468.4 21.3 %collective-permute-start.2 = (bf16[128,2048]{1,0:T(8,128)(2,1)}, bf16[128,2048]{1,0:T(8,128)(2,1)S(1)}, u32[]{:S(2)}, u32[]{:S(2)}) collective-permute-start(bf16[128,2048]{1,0:T(8,128)(2,1)} %get-tuple-element.1251), channel_id=1, source_target_pairs={{0,32},{32,64},{64,96},{96,128},{128,160},{160,192},{192,224},{1,3... | collective-permute-start | bytes 1572872 | tf_op jit(solution)/shard_map/while/body/eval_jaxpr/ppermute | solution.py:29
  589.5 17.8 %collective-permute-start.2 = (bf16[128,2048]{1,0:T(8,128)(2,1)}, bf16[128,2048]{1,0:T(8,128)(2,1)S(1)}, u32[]{:S(2)}, u32[]{:S(2)}) collective-permute-start(bf16[128,2048]{1,0:T(8,128)(2,1)} %get-tuple-element.1251), channel_id=1, source_target_pairs={{0,32},{32,64},{64,96},{96,128},{128,160},{160,192},{192,224},{1,3... | collective-permute-start | bytes 1572872 | tf_op jit(solution)/shard_map/while/body/eval_jaxpr/ppermute | solution.py:29
  641.0 667.8 %while.42 = (s32[]{:T(128)}, bf16[128,2048]{1,0:T(8,128)(2,1)}, bf16[2,128,2048]{2,1,0:T(8,128)(2,1)}, s32[]{:T(128)}, bf16[2,2,128,1024]{3,2,1,0:T(8,128)(2,1)}...) while((s32[]{:T(128)}, bf16[128,2048]{1,0:T(8,128)(2,1)}, ...), condition=%wide.region_24.25_spmd, body=%wide.region_10.24_spmd.sunk | while | flops 3389073152 | bytes 170649296 | solution.py:198
  675.7 15.2 %collective-permute-done.7 = bf16[128,2048]{1,0:T(8,128)(2,1)S(1)} collective-permute-done((bf16[128,2048]{1,0:T(8,128)(2,1)S(1)}, bf16[128,2048]{1,0:T(8,128)(2,1)S(1)}, u32[]{:S(2)}, u32[]{:S(2)}) %collective-permute-start.7) | collective-permute-done | bytes 524320 | tf_op jit(solution)/shard_map/while/body/eval_jaxpr/ppermute | solution.py:29
  726.8 9.4 collective-permute-done.7
  771.0 22.7 %collective-permute-done.7 = bf16[128,2048]{1,0:T(8,128)(2,1)S(1)} collective-permute-done((bf16[128,2048]{1,0:T(8,128)(2,1)S(1)}, bf16[128,2048]{1,0:T(8,128)(2,1)S(1)}, u32[]{:S(2)}, u32[]{:S(2)}) %collective-permute-start.7) | collective-permute-done | bytes 524320 | tf_op jit(solution)/shard_map/while/body/eval_jaxpr/ppermute | solution.py:29
  828.4 9.2 collective-permute-done.7
  872.5 14.1 %collective-permute-done.7 = bf16[128,2048]{1,0:T(8,128)(2,1)S(1)} collective-permute-done((bf16[128,2048]{1,0:T(8,128)(2,1)S(1)}, bf16[128,2048]{1,0:T(8,128)(2,1)S(1)}, u32[]{:S(2)}, u32[]{:S(2)}) %collective-permute-start.7) | collective-permute-done | bytes 524320 | tf_op jit(solution)/shard_map/while/body/eval_jaxpr/ppermute | solution.py:29
  922.3 176.7 %collective-permute-done.7 = bf16[128,2048]{1,0:T(8,128)(2,1)S(1)} collective-permute-done((bf16[128,2048]{1,0:T(8,128)(2,1)S(1)}, bf16[128,2048]{1,0:T(8,128)(2,1)S(1)}, u32[]{:S(2)}, u32[]{:S(2)}) %collective-permute-start.7) | collective-permute-done | bytes 524320 | tf_op jit(solution)/shard_map/while/body/eval_jaxpr/ppermute | solution.py:29
  1111.5 11.2 conditional.10
  1140.7 18.6 %conditional.11 = (bf16[128,2048]{1,0:T(8,128)(2,1)S(1)}) conditional(s32[]{:T(128)} %convert_element_type.302, () %tuple.209, (bf16[2,192,1024]{2,1,0:T(8,128)(2,1)S(1)}, bf16[2,32,1024]{2,1,0:T(8,128)(2,1)S(1)}, bf16[2,32,1024]{2,1,0:T(8,128)(2,1)S(1)}, bf16[2048,1024]{1,0:T(8,128)(2,1)}, bf16[2,128,2048]{2,1,0:T(8,128)(2,1)S(1)}, ...), branch_computations={%region_15.15_spmd, %region_16.23_spmd} | conditional | flops 2693800704 | bytes 90314520 | solution.py:192
  1163.4 9.5 collective-permute-done.7
  1185.4 11.2 conditional.10
  1214.6 18.6 %conditional.11 = (bf16[128,2048]{1,0:T(8,128)(2,1)S(1)}) conditional(s32[]{:T(128)} %convert_element_type.302, () %tuple.209, (bf16[2,192,1024]{2,1,0:T(8,128)(2,1)S(1)}, bf16[2,32,1024]{2,1,0:T(8,128)(2,1)S(1)}, bf16[2,32,1024]{2,1,0:T(8,128)(2,1)S(1)}, bf16[2048,1024]{1,0:T(8,128)(2,1)}, bf16[2,128,2048]{2,1,0:T(8,128)(2,1)S(1)}, ...), branch_computations={%region_15.15_spmd, %region_16.23_spmd} | conditional | flops 2693800704 | bytes 90314520 | solution.py:192
  1237.4 8.6 collective-permute-done.7
  1278.8 27.7 %collective-permute-start.7 = (bf16[128,2048]{1,0:T(8,128)(2,1)S(1)}, bf16[128,2048]{1,0:T(8,128)(2,1)S(1)}, u32[]{:S(2)}, u32[]{:S(2)}) collective-permute-start(bf16[128,2048]{1,0:T(8,128)(2,1)S(1)} %get-tuple-element.1276), channel_id=1, source_target_pairs={{32,0},{64,32},{96,64},{128,96},{160,128},{192,160},{224,192},{33,... | collective-permute-start | bytes 1572872 | tf_op jit(solution)/shard_map/while/body/eval_jaxpr/ppermute | solution.py:29
  (720 shorter events, 651.3 us)
Async XLA Ops:
  7.2 81.8 %all-gather.9.cloned.1.call-start = ((), (), s32[]{:S(2)}) async-start(), calls=%async_computation | async-start | bytes 4325376 | tf_op jit(solution)/shard_map/all_gather | solution.py:101
  7.9 162.8 %all-gather.11.cloned.1.call-start = ((), (), s32[]{:S(2)}) async-start(), calls=%async_computation.1 | async-start | bytes 4325376 | tf_op jit(solution)/shard_map/all_gather | solution.py:102
  8.6 243.8 %all-gather.13.cloned.1.call-start = ((), (), s32[]{:S(2)}) async-start(), calls=%async_computation.2 | async-start | bytes 4325376 | tf_op jit(solution)/shard_map/all_gather | solution.py:103
  9.4 324.7 %all-gather.15.cloned.1.call-start = ((), (), s32[]{:S(2)}) async-start(), calls=%async_computation.3 | async-start | bytes 4325376 | tf_op jit(solution)/shard_map/all_gather | solution.py:104
  350.6 24.1 %collective-permute-start.2 = (bf16[128,2048]{1,0:T(8,128)(2,1)}, bf16[128,2048]{1,0:T(8,128)(2,1)S(1)}, u32[]{:S(2)}, u32[]{:S(2)}) collective-permute-start(bf16[128,2048]{1,0:T(8,128)(2,1)} %get-tuple-element.1251), channel_id=1, source_target_pairs={{0,32},{32,64},{64,96},{96,128},{128,160},{160,192},{192,224},{1,3... | collective-permute-start | bytes 1572872 | tf_op jit(solution)/shard_map/while/body/eval_jaxpr/ppermute | solution.py:29
  443.1 11.4 collective-permute-start.2
  456.0 11.4 collective-permute-start
  468.4 27.8 %collective-permute-start.2 = (bf16[128,2048]{1,0:T(8,128)(2,1)}, bf16[128,2048]{1,0:T(8,128)(2,1)S(1)}, u32[]{:S(2)}, u32[]{:S(2)}) collective-permute-start(bf16[128,2048]{1,0:T(8,128)(2,1)} %get-tuple-element.1251), channel_id=1, source_target_pairs={{0,32},{32,64},{64,96},{96,128},{128,160},{160,192},{192,224},{1,3... | collective-permute-start | bytes 1572872 | tf_op jit(solution)/shard_map/while/body/eval_jaxpr/ppermute | solution.py:29
  497.7 11.4 collective-permute-start
  510.1 11.4 collective-permute-start.2
  523.0 11.4 collective-permute-start
  535.4 14.8 %collective-permute-start.2 = (bf16[128,2048]{1,0:T(8,128)(2,1)}, bf16[128,2048]{1,0:T(8,128)(2,1)S(1)}, u32[]{:S(2)}, u32[]{:S(2)}) collective-permute-start(bf16[128,2048]{1,0:T(8,128)(2,1)} %get-tuple-element.1251), channel_id=1, source_target_pairs={{0,32},{32,64},{64,96},{96,128},{128,160},{160,192},{192,224},{1,3... | collective-permute-start | bytes 1572872 | tf_op jit(solution)/shard_map/while/body/eval_jaxpr/ppermute | solution.py:29
  551.8 11.4 collective-permute-start
  564.2 11.4 collective-permute-start.2
  577.1 11.4 collective-permute-start
  589.5 24.3 %collective-permute-start.2 = (bf16[128,2048]{1,0:T(8,128)(2,1)}, bf16[128,2048]{1,0:T(8,128)(2,1)S(1)}, u32[]{:S(2)}, u32[]{:S(2)}) collective-permute-start(bf16[128,2048]{1,0:T(8,128)(2,1)} %get-tuple-element.1251), channel_id=1, source_target_pairs={{0,32},{32,64},{64,96},{96,128},{128,160},{160,192},{192,224},{1,3... | collective-permute-start | bytes 1572872 | tf_op jit(solution)/shard_map/while/body/eval_jaxpr/ppermute | solution.py:29
  615.3 11.4 collective-permute-start
  627.7 11.4 collective-permute-start.2
  673.8 17.1 %collective-permute-start.7 = (bf16[128,2048]{1,0:T(8,128)(2,1)S(1)}, bf16[128,2048]{1,0:T(8,128)(2,1)S(1)}, u32[]{:S(2)}, u32[]{:S(2)}) collective-permute-start(bf16[128,2048]{1,0:T(8,128)(2,1)S(1)} %get-tuple-element.1276), channel_id=1, source_target_pairs={{32,0},{64,32},{96,64},{128,96},{160,128},{192,160},{224,192},{33,... | collective-permute-start | bytes 1572872 | tf_op jit(solution)/shard_map/while/body/eval_jaxpr/ppermute | solution.py:29
  769.1 24.6 %collective-permute-start.7 = (bf16[128,2048]{1,0:T(8,128)(2,1)S(1)}, bf16[128,2048]{1,0:T(8,128)(2,1)S(1)}, u32[]{:S(2)}, u32[]{:S(2)}) collective-permute-start(bf16[128,2048]{1,0:T(8,128)(2,1)S(1)} %get-tuple-element.1276), channel_id=1, source_target_pairs={{32,0},{64,32},{96,64},{128,96},{160,128},{192,160},{224,192},{33,... | collective-permute-start | bytes 1572872 | tf_op jit(solution)/shard_map/while/body/eval_jaxpr/ppermute | solution.py:29
  870.6 16.0 %collective-permute-start.7 = (bf16[128,2048]{1,0:T(8,128)(2,1)S(1)}, bf16[128,2048]{1,0:T(8,128)(2,1)S(1)}, u32[]{:S(2)}, u32[]{:S(2)}) collective-permute-start(bf16[128,2048]{1,0:T(8,128)(2,1)S(1)} %get-tuple-element.1276), channel_id=1, source_target_pairs={{32,0},{64,32},{96,64},{128,96},{160,128},{192,160},{224,192},{33,... | collective-permute-start | bytes 1572872 | tf_op jit(solution)/shard_map/while/body/eval_jaxpr/ppermute | solution.py:29
  920.3 178.7 %collective-permute-start.7 = (bf16[128,2048]{1,0:T(8,128)(2,1)S(1)}, bf16[128,2048]{1,0:T(8,128)(2,1)S(1)}, u32[]{:S(2)}, u32[]{:S(2)}) collective-permute-start(bf16[128,2048]{1,0:T(8,128)(2,1)S(1)} %get-tuple-element.1276), channel_id=1, source_target_pairs={{32,0},{64,32},{96,64},{128,96},{160,128},{192,160},{224,192},{33,... | collective-permute-start | bytes 1572872 | tf_op jit(solution)/shard_map/while/body/eval_jaxpr/ppermute | solution.py:29
  1161.5 11.5 collective-permute-start.7
  1278.8 29.2 %collective-permute-start.7 = (bf16[128,2048]{1,0:T(8,128)(2,1)S(1)}, bf16[128,2048]{1,0:T(8,128)(2,1)S(1)}, u32[]{:S(2)}, u32[]{:S(2)}) collective-permute-start(bf16[128,2048]{1,0:T(8,128)(2,1)S(1)} %get-tuple-element.1276), channel_id=1, source_target_pairs={{32,0},{64,32},{96,64},{128,96},{160,128},{192,160},{224,192},{33,... | collective-permute-start | bytes 1572872 | tf_op jit(solution)/shard_map/while/body/eval_jaxpr/ppermute | solution.py:29
  (102 other events, 568.7 us)
Sparse Core Ops, SparseCore 0:
  10.6 78.3 all-gather.8
  91.5 79.1 all-gather.10
  173.3 79.1 all-gather.12
  254.9 79.1 all-gather.14
where the time goes:
time: 1320 us
  waiting for transfers between devices  710 us (54%)
  starting transfers between devices  363 us (28%)
  other arithmetic  89.5 us (7%)
  local copies, waits for them, and re-layouts  75.9 us (6%)
  matrix products  59.4 us (4%)
  between operations  13.8 us (1%)
    ppermute x18, waiting for transfers between devices, shifted(): return lax.ppermute(block, axis, route)  301 us
    ppermute x27, starting transfers between devices, padded(): lax.ppermute(lax.slice_in_dim(block, block.shape[dim] - width, None, axis...  191 us
    ppermute x18, starting transfers between devices, shifted(): return lax.ppermute(block, axis, route)  120 us
    select_n x45, other arithmetic, put_slot(): jnp.where(active, lax.dynamic_update_index_in_dim(buffer, value, slot, 0)...  83.1 us
    all_gather x1, waiting for transfers between devices, per_device(): lax.all_gather(w_value[0], 'ctx', axis=0, tiled=True)  81.8 us
    all_gather x1, waiting for transfers between devices, per_device(): lax.all_gather(w_key[0], 'ctx', axis=0, tiled=True)  81.8 us
    all_gather x1, waiting for transfers between devices, per_device(): lax.all_gather(w_out[0], 'ctx', axis=0, tiled=True)  81.6 us
    all_gather x1, waiting for transfers between devices, per_device(): lax.all_gather(w_query[0], 'ctx', axis=0, tiled=True)  78 us
  transfers between devices with their start and end apart: 76, of which 49 were waited for; matrix products, arithmetic and copies ran while one was open for 4% of the time, Pallas kernels for 0%

commit v1 on v0

--- a/solution.py
+++ b/solution.py
@@ -8,6 +8,14 @@
 HDIM = 128
 BLOCKS_DEV = 4
 BLK = 32
+
+
+def tiled_gather(shard, axis, dim):
+    size = lax.axis_size(axis)
+    repeats = [size if d == dim else 1 for d in range(shard.ndim)]
+    return lax.all_to_all(
+        jnp.tile(shard, repeats), axis, split_axis=dim, concat_axis=dim, tiled=True
+    )
 
 
 def padded(block, sides, width):
@@ -98,7 +106,7 @@
     length = section_input.shape[1]
     width = HEADS * HDIM
     full_query, full_key, full_value, full_out = (
-        lax.all_gather(w_query[0], "ctx", axis=0, tiled=True),
+        tiled_gather(w_query[0], "ctx", 0),
         lax.all_gather(w_key[0], "ctx", axis=0, tiled=True),
         lax.all_gather(w_value[0], "ctx", axis=0, tiled=True),
         lax.all_gather(w_out[0], "ctx", axis=0, tiled=True),

time: 1320 us -> 1300 us (0.985)
  waiting for transfers between devices: 710 us -> 691 us
    all_to_all x0 -> x1, waiting for transfers between devices: none -> 116 us  [tiled_gather(): lax.all_to_all(jnp.tile(shard, repeats), axis, split_axis=dim, concat_axi...]
    all_gather x1, waiting for transfers between devices: 81.8 us -> 2.87 us  [per_device(): lax.all_gather(w_key[0], 'ctx', axis=0, tiled=True)]
    all_gather x1 -> x0, waiting for transfers between devices: 78 us -> none  [per_device(): lax.all_gather(w_query[0], 'ctx', axis=0, tiled=True)]
    ppermute x18, waiting for transfers between devices: 301 us -> 328 us  [shifted(): return lax.ppermute(block, axis, route)]
    while x54, local copies, waits for them, and re-layouts: 14.1 us -> 0.48 us
  transfers between devices with their start and end apart: 76 -> 76, of which waited for: 49 -> 49; matrix products, arithmetic and copies ran while one was open for 4% -> 3% of each run, Pallas kernels for 0% -> 0%
where the time goes in v1:
time: 1300 us
  waiting for transfers between devices  691 us (53%)
  starting transfers between devices  376 us (29%)
  other arithmetic  81.4 us (6%)
  local copies, waits for them, and re-layouts  72.8 us (6%)
  matrix products  59.4 us (5%)
  between operations  13.8 us (1%)
    ppermute x18, waiting for transfers between devices, shifted(): return lax.ppermute(block, axis, route)  328 us
    ppermute x27, starting transfers between devices, padded(): lax.ppermute(lax.slice_in_dim(block, block.shape[dim] - width, None, axis...  191 us
    ppermute x18, starting transfers between devices, shifted(): return lax.ppermute(block, axis, route)  123 us
    all_to_all x1, waiting for transfers between devices, tiled_gather(): lax.all_to_all(jnp.tile(shard, repeats), axis, split_axis=dim, concat_axi...  116 us
    all_gather x1, waiting for transfers between devices, per_device(): lax.all_gather(w_out[0], 'ctx', axis=0, tiled=True)  81.8 us
    all_gather x1, waiting for transfers between devices, per_device(): lax.all_gather(w_value[0], 'ctx', axis=0, tiled=True)  78 us
    select_n x45, other arithmetic, put_slot(): jnp.where(active, lax.dynamic_update_index_in_dim(buffer, value, slot, 0)...  71.4 us
    ppermute x27, waiting for transfers between devices, padded(): lax.ppermute(lax.slice_in_dim(block, 0, width, axis=dim), axis, backward)  69 us
  transfers between devices with their start and end apart: 76, of which 49 were waited for; matrix products, arithmetic and copies ran while one was open for 3% of the time, Pallas kernels for 0%

profile of v1, /device:TPU:103, one launch (start us, length us, event | category | flops | bytes accessed | tf_op | source)
XLA Modules:
  0.0 1298.4 jit_solution(17566061720862439847)
XLA Ops:
  12.0 9.8 all-to-all-start
  23.0 115.7 %all-to-all-done = bf16[32,64,1024]{2,1,0:T(8,128)(2,1)} async-done(((bf16[32,64,1024]{2,1,0:T(8,128)(2,1)}), bf16[32,64,1024]{2,1,0:T(8,128)(2,1)}, u32[]{:S(2)}, u32[]{:S(2)}) %all-to-all-start) | async-done | bytes 4194336 | tf_op jit(solution)/shard_map/all_to_all | solution.py:16
  141.5 78.0 %all-gather.9.cloned.1.call-done = bf16[1,2048,1024]{2,1,0:T(8,128)(2,1)} async-done(((bf16[1,64,1024]{2,1,0:T(8,128)(2,1)}), bf16[1,2048,1024]{2,1,0:T(8,128)(2,1)}) %all-gather.9.cloned.1.call-update) | async-done | bytes 4194320 | tf_op jit(solution)/shard_map/all_gather | solution.py:111
  219.5 81.8 %all-gather.11.cloned.1.call-done = bf16[1,1024,2048]{2,1,0:T(8,128)(2,1)} async-done(((bf16[1,32,2048]{2,1,0:T(8,128)(2,1)}), bf16[1,1024,2048]{2,1,0:T(8,128)(2,1)}) %all-gather.11.cloned.1.call-update) | async-done | bytes 4194320 | tf_op jit(solution)/shard_map/all_gather | solution.py:112
  305.4 306.8 %while.41 = (s32[]{:T(128)}, bf16[128,2048]{1,0:T(8,128)(2,1)}, bf16[2,128,2048]{2,1,0:T(8,128)(2,1)S(1)}, bf16[2,128,2048]{2,1,0:T(8,128)(2,1)}, bf16[2,128,102...) while((s32[]{:T(128)}, bf16[128,2048]{1,0:T(8,128)(2,1)}, ...), condition=%wide.region_9.10_spmd, body=%wide.region_0.9_spmd.sunk | while | flops 2211841024 | bytes 80431864 | solution.py:159
  328.9 14.7 %collective-permute-done.2 = bf16[128,2048]{1,0:T(8,128)(2,1)} collective-permute-done((bf16[128,2048]{1,0:T(8,128)(2,1)}, bf16[128,2048]{1,0:T(8,128)(2,1)}, u32[]{:S(2)}, u32[]{:S(2)}) %collective-permute-start.2) | collective-permute-done | bytes 524320 | tf_op jit(solution)/shard_map/while/body/eval_jaxpr/ppermute | solution.py:37
  345.0 10.8 conditional.8
  384.5 10.9 conditional.8
  439.4 22.2 %collective-permute-start.2 = (bf16[128,2048]{1,0:T(8,128)(2,1)}, bf16[128,2048]{1,0:T(8,128)(2,1)}, u32[]{:S(2)}, u32[]{:S(2)}) collective-permute-start(bf16[128,2048]{1,0:T(8,128)(2,1)} %get-tuple-element.1251), channel_id=1, source_target_pairs={{0,32},{32,64},{64,96},{96,128},{128,160},{160,192},{192,224},{1,3... | collective-permute-start | bytes 1572872 | tf_op jit(solution)/shard_map/while/body/eval_jaxpr/ppermute | solution.py:37
  561.6 18.6 %collective-permute-start.2 = (bf16[128,2048]{1,0:T(8,128)(2,1)}, bf16[128,2048]{1,0:T(8,128)(2,1)}, u32[]{:S(2)}, u32[]{:S(2)}) collective-permute-start(bf16[128,2048]{1,0:T(8,128)(2,1)} %get-tuple-element.1251), channel_id=1, source_target_pairs={{0,32},{32,64},{64,96},{96,128},{128,160},{160,192},{192,224},{1,3... | collective-permute-start | bytes 1572872 | tf_op jit(solution)/shard_map/while/body/eval_jaxpr/ppermute | solution.py:37
  613.3 678.6 %while.42 = (s32[]{:T(128)}, bf16[128,2048]{1,0:T(8,128)(2,1)S(1)}, bf16[2,128,2048]{2,1,0:T(8,128)(2,1)}, s32[]{:T(128)}, bf16[2,2,128,1024]{3,2,1,0:T(8,128)(2...) while((s32[]{:T(128)}, bf16[128,2048]{1,0:T(8,128)(2,1)S(1)}, ...), condition=%wide.region_24.25_spmd, body=%wide.region_10.24_spmd.sunk | while | flops 3389073152 | bytes 162784752 | solution.py:206
  648.2 14.5 %collective-permute-done.7 = bf16[128,2048]{1,0:T(8,128)(2,1)S(1)} collective-permute-done((bf16[128,2048]{1,0:T(8,128)(2,1)S(1)}, bf16[128,2048]{1,0:T(8,128)(2,1)S(1)}, u32[]{:S(2)}, u32[]{:S(2)}) %collective-permute-start.7) | collective-permute-done | bytes 524320 | tf_op jit(solution)/shard_map/while/body/eval_jaxpr/ppermute | solution.py:37
  698.4 8.6 collective-permute-done.7
  741.1 24.7 %collective-permute-done.7 = bf16[128,2048]{1,0:T(8,128)(2,1)S(1)} collective-permute-done((bf16[128,2048]{1,0:T(8,128)(2,1)S(1)}, bf16[128,2048]{1,0:T(8,128)(2,1)S(1)}, u32[]{:S(2)}, u32[]{:S(2)}) %collective-permute-start.7) | collective-permute-done | bytes 524320 | tf_op jit(solution)/shard_map/while/body/eval_jaxpr/ppermute | solution.py:37
  799.9 9.5 collective-permute-done.7
  843.5 16.6 %collective-permute-done.7 = bf16[128,2048]{1,0:T(8,128)(2,1)S(1)} collective-permute-done((bf16[128,2048]{1,0:T(8,128)(2,1)S(1)}, bf16[128,2048]{1,0:T(8,128)(2,1)S(1)}, u32[]{:S(2)}, u32[]{:S(2)}) %collective-permute-start.7) | collective-permute-done | bytes 524320 | tf_op jit(solution)/shard_map/while/body/eval_jaxpr/ppermute | solution.py:37
  894.2 186.3 %collective-permute-done.7 = bf16[128,2048]{1,0:T(8,128)(2,1)S(1)} collective-permute-done((bf16[128,2048]{1,0:T(8,128)(2,1)S(1)}, bf16[128,2048]{1,0:T(8,128)(2,1)S(1)}, u32[]{:S(2)}, u32[]{:S(2)}) %collective-permute-start.7) | collective-permute-done | bytes 524320 | tf_op jit(solution)/shard_map/while/body/eval_jaxpr/ppermute | solution.py:37
  1092.2 11.7 conditional.10
  1121.3 20.3 %conditional.11 = (bf16[128,2048]{1,0:T(8,128)(2,1)S(1)}) conditional(s32[]{:T(128)} %convert_element_type.302, () %tuple.209, (bf16[2,192,1024]{2,1,0:T(8,128)(2,1)S(1)}, bf16[2,32,1024]{2,1,0:T(8,128)(2,1)}, bf16[2,32,1024]{2,1,0:T(8,128)(2,1)}, bf16[2048,1024]{1,0:T(8,128)(2,1)}, bf16[2,128,2048]{2,1,0:T(8,128)(2,1)S(1)}, /*index=5*/s32[]{:T(128)}, ...), branch_computations={%region_15.15_spmd, %region_16.23_spmd} | conditional | flops 2693800704 | bytes 88217256 | solution.py:200
  1145.7 9.5 collective-permute-done.7
  1167.0 11.7 conditional.10
  1196.0 20.3 %conditional.11 = (bf16[128,2048]{1,0:T(8,128)(2,1)S(1)}) conditional(s32[]{:T(128)} %convert_element_type.302, () %tuple.209, (bf16[2,192,1024]{2,1,0:T(8,128)(2,1)S(1)}, bf16[2,32,1024]{2,1,0:T(8,128)(2,1)}, bf16[2,32,1024]{2,1,0:T(8,128)(2,1)}, bf16[2048,1024]{1,0:T(8,128)(2,1)}, bf16[2,128,2048]{2,1,0:T(8,128)(2,1)S(1)}, /*index=5*/s32[]{:T(128)}, ...), branch_computations={%region_15.15_spmd, %region_16.23_spmd} | conditional | flops 2693800704 | bytes 88217256 | solution.py:200
  1220.5 8.6 collective-permute-done.7
  1261.2 29.1 %collective-permute-start.7 = (bf16[128,2048]{1,0:T(8,128)(2,1)S(1)}, bf16[128,2048]{1,0:T(8,128)(2,1)S(1)}, u32[]{:S(2)}, u32[]{:S(2)}) collective-permute-start(bf16[128,2048]{1,0:T(8,128)(2,1)S(1)} %get-tuple-element.1276), channel_id=1, source_target_pairs={{32,0},{64,32},{96,64},{128,96},{160,128},{192,160},{224,192},{33,... | collective-permute-start | bytes 1572872 | tf_op jit(solution)/shard_map/while/body/eval_jaxpr/ppermute | solution.py:37
  (706 shorter events, 661.0 us)
Async XLA Ops:
  7.2 134.3 %all-gather.7.cloned.1.call-start = ((), (), s32[]{:S(2)}) async-start(), calls=%async_computation.1 | async-start | bytes 4325376 | tf_op jit(solution)/shard_map/all_gather | solution.py:110
  7.9 211.6 %all-gather.9.cloned.1.call-start = ((), (), s32[]{:S(2)}) async-start(), calls=%async_computation.2 | async-start | bytes 4325376 | tf_op jit(solution)/shard_map/all_gather | solution.py:111
  12.0 126.6 %all-to-all-start = ((bf16[32,64,1024]{2,1,0:T(8,128)(2,1)}), bf16[32,64,1024]{2,1,0:T(8,128)(2,1)}, u32[]{:S(2)}, u32[]{:S(2)}) async-start(bf16[32,64,1024]{2,1,0:T(8,128)(2,1)} %tile.9), calls=%async_computation | async-start | bytes 8388608 | tf_op jit(solution)/shard_map/all_to_all | solution.py:16
  21.9 279.4 %all-gather.11.cloned.1.call-start = ((), (), s32[]{:S(2)}) async-start(), calls=%async_computation.3 | async-start | bytes 4325376 | tf_op jit(solution)/shard_map/all_gather | solution.py:112
  318.7 24.8 %collective-permute-start.2 = (bf16[128,2048]{1,0:T(8,128)(2,1)}, bf16[128,2048]{1,0:T(8,128)(2,1)}, u32[]{:S(2)}, u32[]{:S(2)}) collective-permute-start(bf16[128,2048]{1,0:T(8,128)(2,1)} %get-tuple-element.1251), channel_id=1, source_target_pairs={{0,32},{32,64},{64,96},{96,128},{128,160},{160,192},{192,224},{1,3... | collective-permute-start | bytes 1572872 | tf_op jit(solution)/shard_map/while/body/eval_jaxpr/ppermute | solution.py:37
  413.8 11.5 collective-permute-start.2
  427.0 11.4 collective-permute-start
  439.4 28.6 %collective-permute-start.2 = (bf16[128,2048]{1,0:T(8,128)(2,1)}, bf16[128,2048]{1,0:T(8,128)(2,1)}, u32[]{:S(2)}, u32[]{:S(2)}) collective-permute-start(bf16[128,2048]{1,0:T(8,128)(2,1)} %get-tuple-element.1251), channel_id=1, source_target_pairs={{0,32},{32,64},{64,96},{96,128},{128,160},{160,192},{192,224},{1,3... | collective-permute-start | bytes 1572872 | tf_op jit(solution)/shard_map/while/body/eval_jaxpr/ppermute | solution.py:37
  469.7 11.4 collective-permute-start
  482.1 11.5 collective-permute-start.2
  495.3 11.4 collective-permute-start
  507.7 14.2 %collective-permute-start.2 = (bf16[128,2048]{1,0:T(8,128)(2,1)}, bf16[128,2048]{1,0:T(8,128)(2,1)}, u32[]{:S(2)}, u32[]{:S(2)}) collective-permute-start(bf16[128,2048]{1,0:T(8,128)(2,1)} %get-tuple-element.1251), channel_id=1, source_target_pairs={{0,32},{32,64},{64,96},{96,128},{128,160},{160,192},{192,224},{1,3... | collective-permute-start | bytes 1572872 | tf_op jit(solution)/shard_map/while/body/eval_jaxpr/ppermute | solution.py:37
  523.6 11.4 collective-permute-start
  536.0 11.5 collective-permute-start.2
  549.2 11.4 collective-permute-start
  561.6 25.0 %collective-permute-start.2 = (bf16[128,2048]{1,0:T(8,128)(2,1)}, bf16[128,2048]{1,0:T(8,128)(2,1)}, u32[]{:S(2)}, u32[]{:S(2)}) collective-permute-start(bf16[128,2048]{1,0:T(8,128)(2,1)} %get-tuple-element.1251), channel_id=1, source_target_pairs={{0,32},{32,64},{64,96},{96,128},{128,160},{160,192},{192,224},{1,3... | collective-permute-start | bytes 1572872 | tf_op jit(solution)/shard_map/while/body/eval_jaxpr/ppermute | solution.py:37
  600.6 11.5 collective-permute-start.2
  646.2 16.5 %collective-permute-start.7 = (bf16[128,2048]{1,0:T(8,128)(2,1)S(1)}, bf16[128,2048]{1,0:T(8,128)(2,1)S(1)}, u32[]{:S(2)}, u32[]{:S(2)}) collective-permute-start(bf16[128,2048]{1,0:T(8,128)(2,1)S(1)} %get-tuple-element.1276), channel_id=1, source_target_pairs={{32,0},{64,32},{96,64},{128,96},{160,128},{192,160},{224,192},{33,... | collective-permute-start | bytes 1572872 | tf_op jit(solution)/shard_map/while/body/eval_jaxpr/ppermute | solution.py:37
  739.1 26.6 %collective-permute-start.7 = (bf16[128,2048]{1,0:T(8,128)(2,1)S(1)}, bf16[128,2048]{1,0:T(8,128)(2,1)S(1)}, u32[]{:S(2)}, u32[]{:S(2)}) collective-permute-start(bf16[128,2048]{1,0:T(8,128)(2,1)S(1)} %get-tuple-element.1276), channel_id=1, source_target_pairs={{32,0},{64,32},{96,64},{128,96},{160,128},{192,160},{224,192},{33,... | collective-permute-start | bytes 1572872 | tf_op jit(solution)/shard_map/while/body/eval_jaxpr/ppermute | solution.py:37
  797.9 11.5 collective-permute-start.7
  841.6 18.5 %collective-permute-start.7 = (bf16[128,2048]{1,0:T(8,128)(2,1)S(1)}, bf16[128,2048]{1,0:T(8,128)(2,1)S(1)}, u32[]{:S(2)}, u32[]{:S(2)}) collective-permute-start(bf16[128,2048]{1,0:T(8,128)(2,1)S(1)} %get-tuple-element.1276), channel_id=1, source_target_pairs={{32,0},{64,32},{96,64},{128,96},{160,128},{192,160},{224,192},{33,... | collective-permute-start | bytes 1572872 | tf_op jit(solution)/shard_map/while/body/eval_jaxpr/ppermute | solution.py:37
  892.3 188.2 %collective-permute-start.7 = (bf16[128,2048]{1,0:T(8,128)(2,1)S(1)}, bf16[128,2048]{1,0:T(8,128)(2,1)S(1)}, u32[]{:S(2)}, u32[]{:S(2)}) collective-permute-start(bf16[128,2048]{1,0:T(8,128)(2,1)S(1)} %get-tuple-element.1276), channel_id=1, source_target_pairs={{32,0},{64,32},{96,64},{128,96},{160,128},{192,160},{224,192},{33,... | collective-permute-start | bytes 1572872 | tf_op jit(solution)/shard_map/while/body/eval_jaxpr/ppermute | solution.py:37
  1143.8 11.4 collective-permute-start.7
  1261.2 30.7 %collective-permute-start.7 = (bf16[128,2048]{1,0:T(8,128)(2,1)S(1)}, bf16[128,2048]{1,0:T(8,128)(2,1)S(1)}, u32[]{:S(2)}, u32[]{:S(2)}) collective-permute-start(bf16[128,2048]{1,0:T(8,128)(2,1)S(1)} %get-tuple-element.1276), channel_id=1, source_target_pairs={{32,0},{64,32},{96,64},{128,96},{160,128},{192,160},{224,192},{33,... | collective-permute-start | bytes 1572872 | tf_op jit(solution)/shard_map/while/body/eval_jaxpr/ppermute | solution.py:37
  (95 other events, 723.6 us)
Sparse Core Ops, SparseCore 0:
  10.6 130.8 all-gather.6
  144.1 75.3 all-gather.8
  222.1 79.1 all-gather.10
